TPU v7x, 256 devices: a whole 4x4x8 slice. The times are simulated.
256 devices in a mesh: dp: 32 (over z, y), grp: 8 (over x, core).
Axes of the slice: x: 4, y: 4, z: 8, core: 2. Of those that a mesh axis runs over, the one named last changes fastest.
Arguments:
- tokens: bfloat16 [1024, 256, 1024], P(('dp', 'grp')), may hold values from -0.1875 to 0.1875
- patches: bfloat16 [1024, 256, 1024], P(('dp', 'grp')), may hold values from -0.1875 to 0.1875
- lengths: int32 [1024], P(('dp', 'grp')), may hold values from 16 to 256, as said below
- img_pooled: bfloat16 [1024, 1024], P(('dp', 'grp')), may hold values from -1 to 1
- txt_pooled: bfloat16 [1024, 1024], P(('dp', 'grp')), may hold values from -1 to 1
Outputs:
- grad_tokens: bfloat16 [1024, 256, 1024], P(('dp', 'grp'))
- grad_patches: bfloat16 [1024, 256, 1024], P(('dp', 'grp'))
- grad_img: bfloat16 [1024, 1024], P(('dp', 'grp'))
- grad_txt: bfloat16 [1024, 1024], P(('dp', 'grp'))
- loss_mean: float32 [], replicated
Inputs may be any that keep to these rules, and one draw needn't show every extreme that they name: `lengths`: among the pairs of one index of dp (8 devices along grp), exactly 8 captions have more than 128 tokens; no device holds more than two of them and some device holds two; some caption has exactly 256 tokens and some exactly 128.
All inputs are finite; a program needn't handle non-finite values.
Results may differ from a plain program's by a relative error of at most 0.013.
Values may be sent and summed in bfloat16 or wider, within the bound.
A program may use at most 128 MiB of HBM per device.

v0:
```python
import jax
import jax.numpy as jnp
from jax import lax
from jax.sharding import Mesh
from jax.sharding import PartitionSpec as P

DP_GRP = ("dp_0", "dp_1", "grp_0", "grp_1")
RANGE_EPS = 1e-06
NORM_EPS = 1e-06
GLOBAL_SCALE = 100.0
FINE_SCALE = 50.0
MASK_FILL = -1000000000.0


def side_by_side(arrays, axis, dim, along):
    ends, at = ([], 0)
    for a in arrays[:-1]:
        at += a.shape[along]
        ends.append(at)
    both = jnp.concatenate(arrays, axis=along)
    return tuple(jnp.split(lax.all_gather(both, axis, axis=dim, tiled=True), ends, axis=along))


def gather_turned(arrays, axis, dims):
    turned = [jnp.moveaxis(a, dim, 0) for a, dim in zip(arrays, dims)]
    both = jnp.concatenate([t.reshape(len(t), -1) for t in turned], axis=1)
    filled, at, gathered = (lax.all_gather(both, axis, axis=0, tiled=True), 0, [])
    for t, dim in zip(turned, dims):
        section = filled[:, at : at + t[0].size].reshape(-1, *t.shape[1:])
        gathered.append(jnp.moveaxis(section, 0, dim))
        at += t[0].size
    return tuple(gathered)


def over_axes(array, axes):
    for axis in axes:
        array = lax.psum(array, axis)
    return array


def pair_terms(tok_rows, patch_rows, length):
    patch_count = patch_rows.shape[0]
    slot_count = tok_rows.shape[0]
    similar = jnp.dot(tok_rows, patch_rows.T, preferred_element_type=jnp.float32)
    lowest = jnp.min(similar, 1, keepdims=True)
    highest = jnp.max(similar, 1, keepdims=True)
    scaled = (similar - lowest) / (highest - lowest + RANGE_EPS)
    weights = jnp.maximum(scaled - 1.0 / patch_count, 0.0)
    weights = weights / jnp.sum(weights, 1, keepdims=True)
    grouped = jnp.dot(weights.astype(jnp.bfloat16), patch_rows, preferred_element_type=jnp.float32)
    group_unit = grouped * lax.rsqrt(jnp.sum(grouped * grouped, 1, keepdims=True) + NORM_EPS)
    token_float = tok_rows.astype(jnp.float32)
    token_unit = token_float * lax.rsqrt(
        jnp.sum(token_float * token_float, 1, keepdims=True) + NORM_EPS
    )
    logits = FINE_SCALE * jnp.dot(
        group_unit.astype(jnp.bfloat16),
        token_unit.astype(jnp.bfloat16).T,
        preferred_element_type=jnp.float32,
    )
    position = jnp.arange(slot_count, dtype=jnp.int32)
    valid = position < length
    both_valid = jnp.logical_and(valid[:, None], valid[None, :])
    masked = jnp.where(both_valid, logits, MASK_FILL)
    row_lse = jax.nn.logsumexp(masked, 1)
    col_lse = jax.nn.logsumexp(masked, 0)
    per_token = jnp.where(valid, row_lse + col_lse - 2.0 * jnp.diagonal(logits), 0.0)
    return jnp.sum(per_token) / (2.0 * length.astype(jnp.float32))


def pair_grads(tok_rows, patch_rows, length):

    def closure(first_arg, second_arg):
        return pair_terms(first_arg, second_arg, length)

    value, pullback = jax.vjp(closure, tok_rows, patch_rows)
    grad_tok, grad_patch = pullback(jnp.ones((), jnp.float32))
    return (value, grad_tok, grad_patch)


def fine_block(tok_rows, patch_rows, length_rows):
    return jax.vmap(pair_grads)(tok_rows, patch_rows, length_rows)


def unit_rows(pooled):
    values = pooled.astype(jnp.float32)
    inverse = lax.rsqrt(jnp.sum(values * values, -1, keepdims=True) + NORM_EPS)
    return (values * inverse, inverse)


def body(tokens, patches, lengths, img_pooled, txt_pooled):
    img_unit, img_inverse = unit_rows(img_pooled)
    txt_unit, txt_inverse = unit_rows(txt_pooled)
    img_half = img_unit.astype(jnp.bfloat16)
    txt_half = txt_unit.astype(jnp.bfloat16)
    all_img, all_txt = side_by_side((img_half, txt_half), DP_GRP, 0, 1)
    local_pairs = img_half.shape[0]
    pair_total = all_img.shape[0]
    offset = lax.axis_index(DP_GRP) * local_pairs
    own_mask = (
        jnp.arange(pair_total, dtype=jnp.int32)[None, :]
        == offset + jnp.arange(local_pairs, dtype=jnp.int32)[:, None]
    ).astype(jnp.float32)
    row_logits = GLOBAL_SCALE * jnp.dot(img_half, all_txt.T, preferred_element_type=jnp.float32)
    col_logits = GLOBAL_SCALE * jnp.dot(txt_half, all_img.T, preferred_element_type=jnp.float32)
    row_lse = jax.nn.logsumexp(row_logits, 1)
    col_lse = jax.nn.logsumexp(col_logits, 1)
    matches = GLOBAL_SCALE * jnp.sum(
        img_half.astype(jnp.float32) * txt_half.astype(jnp.float32), -1
    )
    global_part = 0.5 * jnp.sum(row_lse + col_lse - 2.0 * matches)
    row_own = (0.5 * jnp.exp(row_logits - row_lse[:, None]) - 0.5 * own_mask).astype(jnp.bfloat16)
    col_own = (0.5 * jnp.exp(col_logits - col_lse[:, None]) - 0.5 * own_mask).astype(jnp.bfloat16)
    img_local = jnp.dot(row_own, all_txt, preferred_element_type=jnp.float32)
    txt_local = jnp.dot(col_own, all_img, preferred_element_type=jnp.float32)
    lse_rows, lse_cols = gather_turned((row_lse, col_lse), DP_GRP, (0, 0))
    col_rows = (0.5 * jnp.exp(row_logits - lse_cols[None, :]) - 0.5 * own_mask).astype(jnp.bfloat16)
    row_cols = (0.5 * jnp.exp(col_logits - lse_rows[None, :]) - 0.5 * own_mask).astype(jnp.bfloat16)
    img_dir = GLOBAL_SCALE * (
        img_local + jnp.dot(col_rows, all_txt, preferred_element_type=jnp.float32)
    )
    txt_dir = GLOBAL_SCALE * (
        txt_local + jnp.dot(row_cols, all_img, preferred_element_type=jnp.float32)
    )
    grad_img = (
        (img_dir - img_unit * jnp.sum(img_unit * img_dir, -1, keepdims=True)) * img_inverse
    ).astype(jnp.bfloat16)
    grad_txt = (
        (txt_dir - txt_unit * jnp.sum(txt_unit * txt_dir, -1, keepdims=True)) * txt_inverse
    ).astype(jnp.bfloat16)
    values, grad_tokens, grad_patches = fine_block(tokens, patches, lengths)
    summed_loss = over_axes(global_part + jnp.sum(values), DP_GRP)
    loss_mean = summed_loss / pair_total
    return (grad_tokens, grad_patches, grad_img, grad_txt, loss_mean)


def solution(mesh):
    finer = Mesh(mesh.devices.reshape(8, 4, 4, 2), ("dp_0", "dp_1", "grp_0", "grp_1"))
    placed = (
        P(DP_GRP, None, None),
        P(DP_GRP, None, None),
        P(DP_GRP),
        P(DP_GRP, None),
        P(DP_GRP, None),
    )
    return jax.shard_map(
        body,
        mesh=finer,
        in_specs=placed,
        out_specs=(
            P(DP_GRP, None, None),
            P(DP_GRP, None, None),
            P(DP_GRP, None),
            P(DP_GRP, None),
            P(),
        ),
        check_vma=False,
    )
```

profile of v0, /device:TPU:1, one launch (start us, length us, event | category | flops | bytes accessed | tf_op | source)
XLA Modules:
  0.0 264.1 jit_solution(3292715968489793611)
XLA Ops:
  7.2 1.0 fusion.82
  8.2 0.8 fusion.77
  9.0 0.9 multiply_reduce_fusion.2
  9.9 0.6 maximum_bitcast_fusion
  10.6 2.1 fusion.2
  12.7 2.4 fusion.133
  15.1 0.2 maximum_reduce_fusion
  15.3 0.9 multiply_reduce_fusion
  16.3 1.9 copy-done.1
  18.2 2.0 fusion.58
  20.2 16.5 %copy.71 = f32[4,256,256]{0,2,1:T(8,128)} copy(f32[4,256,256]{1,2,0:T(8,128)S(1)} %get-tuple-element.46) | data formatting | bytes 2097152 | tf_op jit(solution)/shard_map/vmap(jvp())/mul | solution.py:56
  36.7 2.3 gather_fusion
  39.1 0.5 fusion.55
  39.7 0.3 fusion.56
  40.0 0.2 fusion.110
  40.2 1.4 and_select_fusion
  41.7 17.4 %copy.65 = f32[4,256,256]{0,2,1:T(8,128)} copy(f32[4,256,256]{1,2,0:T(8,128)} %and_select_fusion) | data formatting | bytes 2097152 | tf_op jit(solution)/shard_map/vmap(transpose(jvp(jit(_where))))/select_n | solution.py:64
  59.1 0.1 copy.66
  59.2 26.1 %scatter_fusion = f32[4,256,256]{0,2,1:T(8,128)} fusion(f32[4,256,256]{0,2,1:T(8,128)} %copy.65, s32[256]{0:T(256)S(1)} %bitcast.34, f32[256,4]{1,0:T(8,128)S(1)} %copy.66), kind=kCustom, calls=%fused_computation.1 | custom fusion | flops 1024 | bytes 14336 | tf_op jit(solution)/shard_map/vmap(transpose(jvp(jit(diagonal))))/cond/branch_0_fun/scatter-add | solution.py:67
  85.3 19.1 %copy.67 = f32[4,256,256]{1,2,0:T(8,128)S(1)} copy(f32[4,256,256]{0,2,1:T(8,128)} %scatter_fusion) | data formatting | bytes 2097152 | tf_op jit(solution)/shard_map/vmap(transpose(jvp(jit(diagonal))))/cond/branch_0_fun/scatter-add | solution.py:67
  104.4 4.3 %fusion = (f32[4,256]{1,0:T(4,128)S(1)}, bf16[4,256,1024]{2,1,0:T(8,128)(2,1)S(1)}) fusion(f32[4,256,1024]{2,1,0:T(8,128)} %copy-done.1, bf16[4,256,1024]{2,1,0:T(8,128)(2,1)} %param.5, f32[4,256]{1,0:T(4,128)S(1)} %get-tuple-element.61, f32[4,256,256]{1,2,0:T(8,128)S(1)} %copy.67), kind=kOutput, calls=%fused_computation.11 | convolution fusion | flops 544472064 | bytes 9445376 | tf_op jit(solution)/shard_map/vmap(transpose(jvp()))/dot_general | solution.py:56
  108.7 0.3 copy-done.7
  109.0 2.2 fusion.52
  111.2 0.6 divide_reduce_fusion
  111.8 4.3 %fusion.4 = (f32[4,256]{1,0:T(4,128)S(1)}, bf16[4,256,1024]{2,1,0:T(8,128)(2,1)S(1)}) fusion(bf16[4,256,1024]{2,1,0:T(8,128)(2,1)} %param.5, f32[4,256,1024]{2,1,0:T(8,128)} %copy-done.1, f32[4,256]{1,0:T(4,128)S(1)} %get-tuple-element.62, f32[4,256,256]{1,2,0:T(8,128)S(1)} %copy.67), kind=kOutput, calls=%fused_computation.15 | convolution fusion | flops 544472064 | bytes 9445376 | tf_op jit(solution)/shard_map/vmap(transpose(jvp()))/dot_general | solution.py:56
  116.1 1.0 fusion.131
  117.3 1.6 fusion.5
  118.9 2.1 convert_add_fusion
  121.0 2.6 fusion.7
  123.7 7.9 %all-gather.4.cloned.1.call-done = bf16[256,4,2048]{2,1,0:T(4,128)(2,1)} async-done(((bf16[1,4,2048]{2,1,0:T(4,128)(2,1)}), bf16[256,4,2048]{2,1,0:T(4,128)(2,1)}) %all-gather.4.cloned.1.call-update) | async-done | bytes 4194320 | tf_op jit(solution)/shard_map/all_gather | solution.py:21
  131.5 6.9 %reshape.209 = bf16[1024,2048]{1,0:T(8,128)(2,1)} reshape(bf16[256,4,2048]{2,1,0:T(4,128)(2,1)} %all-gather.4.cloned.1.call-done) | data formatting | bytes 8388608
  138.4 2.3 fusion.141
  140.8 2.4 fusion.140
  143.2 0.2 exponential_reduce_fusion
  143.4 0.2 exponential_reduce_fusion.1
  143.6 60.9 %all-gather.1 = f32[256,4,2]{1,2,0:T(2,128)S(1)} all-gather(f32[1,4,2]{1,2,0:T(2,128)S(1)} %maximum_bitcast_fusion.1), channel_id=1, replica_groups=mesh['dp_0'=8,'dp_1'=4,'grp_0'=4,'grp_1'=2] {'dp_0','dp_1','grp_0','grp_1'}, dimensions={0}, use_global_device_ids=true | all-gather | bytes 8224 | tf_op jit(solution)/shard_map/all_gather | solution.py:27
  204.5 0.6 subtract_reduce_fusion
  206.5 12.9 %psum.28 = f32[]{:T(128)} all-reduce(f32[]{:T(128)S(6)} %add.150), channel_id=1, replica_groups=mesh['dp_0'=8,'dp_1'=4,'grp_0'=4,'grp_1'=2] {'dp_0'}, use_global_device_ids=true, to_apply=%region_29.30 | all-reduce | flops 1 | bytes 8 | tf_op jit(solution)/shard_map/psum | solution.py:37
  219.3 0.2 reshape.211
  219.5 7.9 %psum.29 = f32[]{:T(128)} all-reduce(f32[]{:T(128)} %psum.28), channel_id=1, replica_groups=mesh['dp_0'=8,'dp_1'=4,'grp_0'=4,'grp_1'=2] {'dp_1'}, use_global_device_ids=true, to_apply=%region_30.31 | all-reduce | flops 1 | bytes 8 | tf_op jit(solution)/shard_map/psum | solution.py:37
  227.4 8.0 %psum.30 = f32[]{:T(128)} all-reduce(f32[]{:T(128)} %psum.29), channel_id=1, replica_groups=mesh['dp_0'=8,'dp_1'=4,'grp_0'=4,'grp_1'=2] {'grp_0'}, use_global_device_ids=true, to_apply=%region_31.32 | all-reduce | flops 1 | bytes 8 | tf_op jit(solution)/shard_map/psum | solution.py:37
  235.4 2.0 fusion.21
  237.4 2.0 fusion.15
  239.4 10.4 %psum.31 = f32[]{:T(128)} all-reduce(f32[]{:T(128)} %psum.30), channel_id=1, replica_groups=mesh['dp_0'=8,'dp_1'=4,'grp_0'=4,'grp_1'=2] {'grp_1'}, use_global_device_ids=true, to_apply=%region_32.33 | all-reduce | flops 1 | bytes 8 | tf_op jit(solution)/shard_map/psum | solution.py:37
  249.8 2.1 fusion.73
  251.9 0.7 fusion.76
  252.6 2.1 fusion.78
  254.8 0.7 fusion.81
  (54 shorter events, 0.6 us)
Async XLA Ops:
  7.2 5.5 %copy-start = (bf16[4,256,1024]{2,1,0:T(8,128)(2,1)S(1)}, bf16[4,256,1024]{2,1,0:T(8,128)(2,1)}, u32[]{:S(2)}) copy-start(bf16[4,256,1024]{2,1,0:T(8,128)(2,1)} %param.6) | copy-start | bytes 6291460
  7.2 7.8 %copy-start.14 = (s32[4]{0:T(128)S(1)}, s32[4]{0:T(128)}, u32[]{:S(2)}) copy-start(s32[4]{0:T(128)} %param.7) | copy-start | bytes 52
  7.2 124.3 %all-gather.4.cloned.1.call-start = ((), (), s32[]{:S(2)}) async-start(), calls=%async_computation | async-start | bytes 4210688 | tf_op jit(solution)/shard_map/all_gather | solution.py:21
  15.0 1.2 copy-start.6
  15.3 2.9 %copy-start.4 = (bf16[4,256,1024]{2,1,0:T(8,128)(2,1)S(1)}, bf16[4,256,1024]{2,1,0:T(8,128)(2,1)}, u32[]{:S(2)}) copy-start(bf16[4,256,1024]{2,1,0:T(8,128)(2,1)} %param.5) | copy-start | bytes 6291460
  16.3 1.9 copy-start.1
  104.4 4.4 %copy-start.2 = (f32[4,256,1024]{2,1,0:T(8,128)S(1)}, f32[4,256,1024]{2,1,0:T(8,128)}, u32[]{:S(2)}) copy-start(f32[4,256,1024]{2,1,0:T(8,128)} %copy-done.1) | copy-start | bytes 12582916
  104.4 4.6 %copy-start.7 = (f32[4,256,256]{1,2,0:T(8,128)S(1)}, f32[4,256,256]{1,2,0:T(8,128)}, u32[]{:S(2)}) copy-start(f32[4,256,256]{1,2,0:T(8,128)} %copy-done.6) | copy-start | bytes 3145732
  108.7 2.5 copy-start.9
  111.8 4.3 %copy-start.8 = (f32[4,256,256]{1,2,0:T(8,128)S(1)}, f32[4,256,256]{1,2,0:T(8,128)}, u32[]{:S(2)}) copy-start(f32[4,256,256]{1,2,0:T(8,128)} %copy-done.6) | copy-start | bytes 3145732
  111.8 4.3 %copy-start.11 = (bf16[4,256,256]{1,2,0:T(8,128)(2,1)S(1)}, bf16[4,256,256]{1,2,0:T(8,128)(2,1)}, u32[]{:S(2)}) copy-start(bf16[4,256,256]{1,2,0:T(8,128)(2,1)} %get-tuple-element.52) | copy-start | bytes 1572868
  111.8 5.3 %copy-start.3 = (f32[4,256,1024]{2,1,0:T(8,128)S(1)}, f32[4,256,1024]{2,1,0:T(8,128)}, u32[]{:S(2)}) copy-start(f32[4,256,1024]{2,1,0:T(8,128)} %copy-done.1) | copy-start | bytes 12582916
  111.8 5.5 %copy-start.10 = (bf16[4,256,1024]{2,1,0:T(8,128)(2,1)S(1)}, bf16[4,256,1024]{2,1,0:T(8,128)(2,1)}, u32[]{:S(2)}) copy-start(bf16[4,256,1024]{2,1,0:T(8,128)(2,1)} %copy-done.9) | copy-start | bytes 6291460
  117.3 1.6 copy-start.5
  140.8 109.0 %copy-start.12 = (bf16[4,1024]{1,0:T(4,128)(2,1)S(1)}, bf16[4,1024]{1,0:T(4,128)(2,1)}, u32[]{:S(2)}) copy-start(bf16[4,1024]{1,0:T(4,128)(2,1)} %param.8) | copy-start | bytes 24580
  143.1 109.5 %copy-start.13 = (bf16[4,1024]{1,0:T(4,128)(2,1)S(1)}, bf16[4,1024]{1,0:T(4,128)(2,1)}, u32[]{:S(2)}) copy-start(bf16[4,1024]{1,0:T(4,128)(2,1)} %param.9) | copy-start | bytes 24580
Sparse Core Ops, SparseCore 0:
  11.6 119.8 all-gather.3
where the time goes:
time: 266 us; the launch traced here: 264 us
  blocking collectives  100 us (38%)
  local copies, waits for them, and re-layouts  64.9 us (24%)
  other arithmetic  38.3 us (14%)
  matrix products  35.4 us (13%)
  between operations  17.4 us (7%)
  waiting for transfers between devices  7.87 us (3%)
    all_gather x1, blocking collectives, gather_turned(): lax.all_gather(both, axis, axis=0, tiled=True)  60.9 us
    psum x4, blocking collectives, over_axes(): array = lax.psum(array, axis)  39.1 us
    scatter-add x1, other arithmetic, pair_terms(): jnp.diagonal(logits)  26.1 us
    scatter-add x1, local copies, waits for them, and re-layouts, pair_terms(): jnp.diagonal(logits)  19.1 us
    select_n x1, local copies, waits for them, and re-layouts, pair_terms(): masked = jnp.where(both_valid, logits, MASK_FILL)  17.4 us
    mul x1, local copies, waits for them, and re-layouts, pair_terms(): FINE_SCALE * jnp.dot(group_unit.astype(jnp.bfloat16), token_unit.astype(j...  16.5 us
    dot_general x3, matrix products, pair_terms(): jnp.dot(group_unit.astype(jnp.bfloat16), token_unit.astype(jnp.bfloat16)....  10.6 us
    unnamed x33, local copies, waits for them, and re-layouts  9.52 us
  transfers between devices with their start and end apart: 1, of which 1 were waited for; matrix products, arithmetic and copies ran while one was open for 42% of the time, Pallas kernels for 0%

commit v1 on v0

--- a/solution.py
+++ b/solution.py
@@ -24,7 +24,13 @@
 def gather_turned(arrays, axis, dims):
     turned = [jnp.moveaxis(a, dim, 0) for a, dim in zip(arrays, dims)]
     both = jnp.concatenate([t.reshape(len(t), -1) for t in turned], axis=1)
-    filled, at, gathered = (lax.all_gather(both, axis, axis=0, tiled=True), 0, [])
+    filled, at, gathered = (
+        jnp.concatenate(
+            lax.all_to_all(jnp.stack([both] * lax.axis_size(axis)), axis, 0, 0), axis=0
+        ),
+        0,
+        [],
+    )
     for t, dim in zip(turned, dims):
         section = filled[:, at : at + t[0].size].reshape(-1, *t.shape[1:])
         gathered.append(jnp.moveaxis(section, 0, dim))

time: 266 us -> 213 us (0.80)
  blocking collectives: 100 us -> 36 us
  starting transfers between devices: 0.04 us -> 13.4 us
  matrix products: 35.4 us -> 32.4 us
    all_gather x1 -> x0, blocking collectives: 60.9 us -> none  [gather_turned(): lax.all_gather(both, axis, axis=0, tiled=True)]
    all_to_all x0 -> x1, starting transfers between devices: none -> 13.3 us  [gather_turned(): lax.all_to_all(jnp.stack([both] * lax.axis_size(axis)), axis, 0, 0)]
    psum x4, blocking collectives: 39.1 us -> 36 us  [over_axes(): array = lax.psum(array, axis)]
    unnamed x33 -> x34, local copies, waits for them, and re-layouts: 9.52 us -> 9.37 us
  transfers between devices with their start and end apart: 1 -> 2, of which waited for: 1 -> 2; matrix products, arithmetic and copies ran while one was open for 42% -> 52% of each run, Pallas kernels for 0% -> 0%
where the time goes in v1:
time: 213 us; the launch traced here: 211 us
  local copies, waits for them, and re-layouts  65.7 us (31%)
  other arithmetic  38.3 us (18%)
  blocking collectives  36 us (17%)
  matrix products  32.4 us (15%)
  between operations  17.4 us (8%)
  starting transfers between devices  13.4 us (6%)
  waiting for transfers between devices  8.13 us (4%)
    psum x4, blocking collectives, over_axes(): array = lax.psum(array, axis)  36 us
    scatter-add x1, other arithmetic, pair_terms(): jnp.diagonal(logits)  26.1 us
    scatter-add x1, local copies, waits for them, and re-layouts, pair_terms(): jnp.diagonal(logits)  19.1 us
    select_n x1, local copies, waits for them, and re-layouts, pair_terms(): masked = jnp.where(both_valid, logits, MASK_FILL)  17.4 us
    mul x1, local copies, waits for them, and re-layouts, pair_terms(): FINE_SCALE * jnp.dot(group_unit.astype(jnp.bfloat16), token_unit.astype(j...  16.5 us
    all_to_all x1, starting transfers between devices, gather_turned(): lax.all_to_all(jnp.stack([both] * lax.axis_size(axis)), axis, 0, 0)  13.3 us
    dot_general x3, matrix products, pair_terms(): jnp.dot(group_unit.astype(jnp.bfloat16), token_unit.astype(jnp.bfloat16)....  10.6 us
    unnamed x34, local copies, waits for them, and re-layouts  9.37 us
  transfers between devices with their start and end apart: 2, of which 2 were waited for; matrix products, arithmetic and copies ran while one was open for 52% of the time, Pallas kernels for 0%

profile of v1, /device:TPU:1, one launch (start us, length us, event | category | flops | bytes accessed | tf_op | source)
XLA Modules:
  0.0 211.4 jit_solution(7068607797184535583)
XLA Ops:
  7.2 1.0 fusion.82
  8.2 0.8 fusion.77
  9.0 0.9 multiply_reduce_fusion.2
  9.9 0.6 maximum_bitcast_fusion
  10.6 2.1 fusion.2
  12.7 2.4 %fusion.133 = (f32[4,256]{1,0:T(4,128)S(1)}, f32[4,256]{1,0:T(4,128)S(1)}, f32[4,256,256]{1,2,0:T(8,128)S(1)}) fusion(bf16[4,256,1024]{2,1,0:T(8,128)(2,1)} %param.5, bf16[4,256,1024]{2,1,0:T(8,128)(2,1)S(1)} %copy-done), kind=kOutput, calls=%fused_computation.192 | convolution fusion | flops 537393152 | bytes 5251072 | tf_op jit(solution)/shard_map/vmap(jvp())/dot_general | solution.py:50
  15.0 0.2 maximum_reduce_fusion
  15.3 0.9 multiply_reduce_fusion
  16.3 1.9 copy-done.2
  18.2 2.0 fusion.58
  20.2 16.5 %copy.84 = f32[4,256,256]{0,2,1:T(8,128)} copy(f32[4,256,256]{1,2,0:T(8,128)S(1)} %get-tuple-element.46) | data formatting | bytes 2097152 | tf_op jit(solution)/shard_map/vmap(jvp())/mul | solution.py:62
  36.7 2.3 %gather_fusion = f32[256,4]{1,0:T(8,128)S(1)} fusion(f32[4,256,256]{0,2,1:T(8,128)} %copy.84, s32[256]{0:T(256)S(1)} %bitcast.33), kind=kCustom, calls=%fused_computation | custom fusion | bytes 10240 | tf_op jit(solution)/shard_map/vmap(jvp(jit(diagonal)))/cond/branch_0_fun/gather | solution.py:73
  39.1 0.5 fusion.55
  39.7 0.3 fusion.56
  40.0 0.2 fusion.110
  40.2 1.4 and_select_fusion
  41.6 17.4 %copy.78 = f32[4,256,256]{0,2,1:T(8,128)} copy(f32[4,256,256]{1,2,0:T(8,128)} %and_select_fusion) | data formatting | bytes 2097152 | tf_op jit(solution)/shard_map/vmap(transpose(jvp(jit(_where))))/select_n | solution.py:70
  59.2 26.1 %scatter_fusion = f32[4,256,256]{0,2,1:T(8,128)} fusion(f32[4,256,256]{0,2,1:T(8,128)} %copy.78, s32[256]{0:T(256)S(1)} %bitcast.32, f32[256,4]{1,0:T(8,128)S(1)} %copy.79), kind=kCustom, calls=%fused_computation.1 | custom fusion | flops 1024 | bytes 14336 | tf_op jit(solution)/shard_map/vmap(transpose(jvp(jit(diagonal))))/cond/branch_0_fun/scatter-add | solution.py:73
  85.2 19.1 %copy.80 = f32[4,256,256]{1,2,0:T(8,128)S(1)} copy(f32[4,256,256]{0,2,1:T(8,128)} %scatter_fusion) | data formatting | bytes 2097152 | tf_op jit(solution)/shard_map/vmap(transpose(jvp(jit(diagonal))))/cond/branch_0_fun/scatter-add | solution.py:73
  104.3 4.3 %fusion = (f32[4,256]{1,0:T(4,128)S(1)}, bf16[4,256,1024]{2,1,0:T(8,128)(2,1)S(1)}) fusion(f32[4,256,1024]{2,1,0:T(8,128)} %copy-done.2, bf16[4,256,1024]{2,1,0:T(8,128)(2,1)} %param.5, f32[4,256]{1,0:T(4,128)S(1)} %get-tuple-element.61, f32[4,256,256]{1,2,0:T(8,128)S(1)} %copy.80), kind=kOutput, calls=%fused_computation.11 | convolution fusion | flops 544472064 | bytes 9445376 | tf_op jit(solution)/shard_map/vmap(transpose(jvp()))/dot_general | solution.py:62
  108.7 0.3 copy-done.8
  108.9 2.2 %fusion.52 = (f32[4,256]{1,0:T(4,128)S(1)}, bf16[4,256,256]{1,2,0:T(8,128)(2,1)}) fusion(f32[4,256]{1,0:T(4,128)S(1)} %multiply_divide_fusion.1, f32[4,256]{1,0:T(4,128)S(1)} %get-tuple-element.27, f32[4,256,256]{1,2,0:T(8,128)S(1)} %copy-done.8, f32[4,256]{1,0:T(4,128)S(1)} %get-tuple-element.15, bf16[4,256,1024]{2,1,0:T(8,128)(2,1)S(1)} %copy-done, ...), kind=kOutput, calls=%fused_computation.56 | convolution fusion | flops 544472064 | bytes 9986048 | tf_op jit(solution)/shard_map/vmap(transpose(jvp()))/dot_general | solution.py:56
  111.2 0.6 divide_reduce_fusion
  111.8 4.3 %fusion.4 = (f32[4,256]{1,0:T(4,128)S(1)}, bf16[4,256,1024]{2,1,0:T(8,128)(2,1)S(1)}) fusion(bf16[4,256,1024]{2,1,0:T(8,128)(2,1)} %param.5, f32[4,256,1024]{2,1,0:T(8,128)} %copy-done.2, f32[4,256]{1,0:T(4,128)S(1)} %get-tuple-element.62, f32[4,256,256]{1,2,0:T(8,128)S(1)} %copy.80), kind=kOutput, calls=%fused_computation.15 | convolution fusion | flops 544472064 | bytes 9445376 | tf_op jit(solution)/shard_map/vmap(transpose(jvp()))/dot_general | solution.py:62
  116.1 1.0 fusion.131
  117.3 1.6 fusion.5
  118.9 2.1 %convert_add_fusion = bf16[4,256,1024]{2,1,0:T(8,128)(2,1)} fusion(bf16[4,256,1024]{2,1,0:T(8,128)(2,1)S(1)} %fusion.5, bf16[4,256,1024]{2,1,0:T(8,128)(2,1)S(1)} %copy-done.6, pred[4,256,256]{1,2,0:T(32,128)(4,1)S(1)} %get-tuple-element.31, pred[4,256,256]{1,2,0:T(32,128)(4,1)S(1)} %get-tuple-element.33, f32[4,256]{1,0:T(4,128)S(1)} %get-tuple-element.40, ...), kind=kOutput, calls=%fused_computation.21 | convolution fusion | flops 540278784 | bytes 7876608 | tf_op jit(solution)/shard_map/vmap(transpose(jvp()))/dot_general | solution.py:50
  121.0 2.6 %fusion.7 = bf16[4,256,1024]{2,1,0:T(8,128)(2,1)} fusion(bf16[4,256,1024]{2,1,0:T(8,128)(2,1)S(1)} %copy-done.6, bf16[4,256,1024]{2,1,0:T(8,128)(2,1)S(1)} %get-tuple-element.48, f32[4,256]{1,0:T(4,128)S(1)} %multiply_multiply_fusion.1, f32[4,256]{1,0:T(4,128)S(1)} %get-tuple-element.61, bf16[4,256,1024]{2,1,0:T(8,128)(2,1)S(1)} %copy-done, ...), kind=kOutput, calls=%fused_computation.20 | convolution fusion | flops 547618816 | bytes 9981952 | tf_op jit(solution)/shard_map/vmap(transpose(jvp()))/dot_general | solution.py:50
  123.6 7.9 %all-gather.3.cloned.1.call-done = bf16[256,4,2048]{2,1,0:T(4,128)(2,1)} async-done(((bf16[1,4,2048]{2,1,0:T(4,128)(2,1)}), bf16[256,4,2048]{2,1,0:T(4,128)(2,1)}) %all-gather.3.cloned.1.call-update) | async-done | bytes 4194320 | tf_op jit(solution)/shard_map/all_gather | solution.py:21
  131.5 6.9 %reshape.215 = bf16[1024,2048]{1,0:T(8,128)(2,1)} reshape(bf16[256,4,2048]{2,1,0:T(4,128)(2,1)} %all-gather.3.cloned.1.call-done) | data formatting | bytes 8388608
  138.4 2.3 %fusion.141 = (f32[4]{0:T(128)S(1)}, f32[4,1024]{1,0:T(4,128)S(1)}) fusion(bf16[4,1024]{1,0:T(4,128)(2,1)S(1)} %get-tuple-element.21, bf16[1024,2048]{1,0:T(8,128)(2,1)} %reshape.215), kind=kOutput, calls=%fused_computation.195 | convolution fusion | flops 8396796 | bytes 2121744 | tf_op jit(solution)/shard_map/dot_general | solution.py:110
  140.8 2.4 %fusion.140 = (f32[4]{0:T(128)S(1)}, f32[4,1024]{1,0:T(4,128)S(1)}) fusion(bf16[4,1024]{1,0:T(4,128)(2,1)S(1)} %get-tuple-element.22, bf16[1024,2048]{1,0:T(8,128)(2,1)} %reshape.215), kind=kOutput, calls=%fused_computation.194 | convolution fusion | flops 8396796 | bytes 2121744 | tf_op jit(solution)/shard_map/dot_general | solution.py:111
  143.2 0.2 exponential_reduce_fusion
  143.4 0.2 exponential_reduce_fusion.1
  143.6 0.6 subtract_reduce_fusion
  145.5 13.0 %psum.28 = f32[]{:T(128)} all-reduce(f32[]{:T(128)S(6)} %add.150), channel_id=1, replica_groups=mesh['dp_0'=8,'dp_1'=4,'grp_0'=4,'grp_1'=2] {'dp_0'}, use_global_device_ids=true, to_apply=%region_29.30 | all-reduce | flops 1 | bytes 8 | tf_op jit(solution)/shard_map/psum | solution.py:43
  158.5 8.7 %psum.29 = f32[]{:T(128)} all-reduce(f32[]{:T(128)} %psum.28), channel_id=1, replica_groups=mesh['dp_0'=8,'dp_1'=4,'grp_0'=4,'grp_1'=2] {'dp_1'}, use_global_device_ids=true, to_apply=%region_30.31 | all-reduce | flops 1 | bytes 8 | tf_op jit(solution)/shard_map/psum | solution.py:43
  167.2 0.8 stack.2
  167.9 13.3 %all-to-all-start = ((f32[256,4,2]{1,2,0:T(2,128)}), f32[256,4,2]{1,2,0:T(2,128)S(1)}, u32[]{:S(2)}, u32[]{:S(2)}) async-start(f32[256,4,2]{1,2,0:T(2,128)} %stack.2), calls=%async_computation | async-start | bytes 524288 | tf_op jit(solution)/shard_map/all_to_all | solution.py:29
  181.2 9.8 %psum.30 = f32[]{:T(128)} all-reduce(f32[]{:T(128)} %psum.29), channel_id=1, replica_groups=mesh['dp_0'=8,'dp_1'=4,'grp_0'=4,'grp_1'=2] {'grp_0'}, use_global_device_ids=true, to_apply=%region_31.32 | all-reduce | flops 1 | bytes 8 | tf_op jit(solution)/shard_map/psum | solution.py:43
  191.0 4.6 %psum.31 = f32[]{:T(128)} all-reduce(f32[]{:T(128)} %psum.30), channel_id=1, replica_groups=mesh['dp_0'=8,'dp_1'=4,'grp_0'=4,'grp_1'=2] {'grp_1'}, use_global_device_ids=true, to_apply=%region_32.33 | all-reduce | flops 1 | bytes 8 | tf_op jit(solution)/shard_map/psum | solution.py:43
  196.3 0.3 all-to-all-done
  196.7 2.2 %fusion.21 = f32[4,1024]{1,0:T(4,128)S(1)} fusion(bf16[1024,2048]{1,0:T(8,128)(2,1)} %reshape.215, f32[4,1024]{1,0:T(4,128)S(1)} %get-tuple-element.56, f32[1024]{0:T(1024)S(1)} %bitcast.35, s32[4]{0:T(128)S(1)} %iota_add_fusion), kind=kOutput, calls=%fused_computation.35 | convolution fusion | flops 8413184 | bytes 2134032 | tf_op jit(solution)/shard_map/dot_general | solution.py:126
  198.9 2.0 fusion.15
  200.9 0.5 fusion.73
  201.5 0.7 fusion.76
  202.2 0.5 fusion.78
  202.7 0.7 fusion.81
  (58 shorter events, 0.9 us)
Async XLA Ops:
  7.2 5.5 %copy-start = (bf16[4,256,1024]{2,1,0:T(8,128)(2,1)S(1)}, bf16[4,256,1024]{2,1,0:T(8,128)(2,1)}, u32[]{:S(2)}) copy-start(bf16[4,256,1024]{2,1,0:T(8,128)(2,1)} %param.6) | copy-start | bytes 6291460
  7.2 124.3 %all-gather.3.cloned.1.call-start = ((), (), s32[]{:S(2)}) async-start(), calls=%async_computation.1 | async-start | bytes 4210688 | tf_op jit(solution)/shard_map/all_gather | solution.py:21
  10.6 4.7 %copy-start.15 = (s32[4]{0:T(128)S(1)}, s32[4]{0:T(128)}, u32[]{:S(2)}) copy-start(s32[4]{0:T(128)} %param.7) | copy-start | bytes 52
  15.0 1.2 copy-start.7
  15.3 2.9 %copy-start.5 = (bf16[4,256,1024]{2,1,0:T(8,128)(2,1)S(1)}, bf16[4,256,1024]{2,1,0:T(8,128)(2,1)}, u32[]{:S(2)}) copy-start(bf16[4,256,1024]{2,1,0:T(8,128)(2,1)} %param.5) | copy-start | bytes 6291460
  16.2 1.9 copy-start.2
  104.3 4.3 %copy-start.3 = (f32[4,256,1024]{2,1,0:T(8,128)S(1)}, f32[4,256,1024]{2,1,0:T(8,128)}, u32[]{:S(2)}) copy-start(f32[4,256,1024]{2,1,0:T(8,128)} %copy-done.2) | copy-start | bytes 12582916
  104.3 4.6 %copy-start.8 = (f32[4,256,256]{1,2,0:T(8,128)S(1)}, f32[4,256,256]{1,2,0:T(8,128)}, u32[]{:S(2)}) copy-start(f32[4,256,256]{1,2,0:T(8,128)} %copy-done.7) | copy-start | bytes 3145732
  108.6 2.5 %copy-start.10 = (bf16[4,256,1024]{2,1,0:T(8,128)(2,1)}, bf16[4,256,1024]{2,1,0:T(8,128)(2,1)S(1)}, u32[]{:S(2)}) copy-start(bf16[4,256,1024]{2,1,0:T(8,128)(2,1)S(1)} %get-tuple-element.50) | copy-start | bytes 6291460
  111.8 4.3 %copy-start.9 = (f32[4,256,256]{1,2,0:T(8,128)S(1)}, f32[4,256,256]{1,2,0:T(8,128)}, u32[]{:S(2)}) copy-start(f32[4,256,256]{1,2,0:T(8,128)} %copy-done.7) | copy-start | bytes 3145732
  111.8 4.3 %copy-start.12 = (bf16[4,256,256]{1,2,0:T(8,128)(2,1)S(1)}, bf16[4,256,256]{1,2,0:T(8,128)(2,1)}, u32[]{:S(2)}) copy-start(bf16[4,256,256]{1,2,0:T(8,128)(2,1)} %get-tuple-element.52) | copy-start | bytes 1572868
  111.8 5.4 %copy-start.4 = (f32[4,256,1024]{2,1,0:T(8,128)S(1)}, f32[4,256,1024]{2,1,0:T(8,128)}, u32[]{:S(2)}) copy-start(f32[4,256,1024]{2,1,0:T(8,128)} %copy-done.2) | copy-start | bytes 12582916
  111.8 5.5 %copy-start.11 = (bf16[4,256,1024]{2,1,0:T(8,128)(2,1)S(1)}, bf16[4,256,1024]{2,1,0:T(8,128)(2,1)}, u32[]{:S(2)}) copy-start(bf16[4,256,1024]{2,1,0:T(8,128)(2,1)} %copy-done.10) | copy-start | bytes 6291460
  117.3 1.6 copy-start.6
  140.8 60.2 %copy-start.13 = (bf16[4,1024]{1,0:T(4,128)(2,1)S(1)}, bf16[4,1024]{1,0:T(4,128)(2,1)}, u32[]{:S(2)}) copy-start(bf16[4,1024]{1,0:T(4,128)(2,1)} %param.8) | copy-start | bytes 24580
  143.1 59.0 %copy-start.14 = (bf16[4,1024]{1,0:T(4,128)(2,1)S(1)}, bf16[4,1024]{1,0:T(4,128)(2,1)}, u32[]{:S(2)}) copy-start(bf16[4,1024]{1,0:T(4,128)(2,1)} %param.9) | copy-start | bytes 24580
  167.9 28.6 %all-to-all-start = ((f32[256,4,2]{1,2,0:T(2,128)}), f32[256,4,2]{1,2,0:T(2,128)S(1)}, u32[]{:S(2)}, u32[]{:S(2)}) async-start(f32[256,4,2]{1,2,0:T(2,128)} %stack.2), calls=%async_computation | async-start | bytes 524288 | tf_op jit(solution)/shard_map/all_to_all | solution.py:29
  196.7 4.2 %copy-start.1 = (bf16[1024,2048]{1,0:T(8,128)(2,1)S(1)}, bf16[1024,2048]{1,0:T(8,128)(2,1)}, u32[]{:S(2)}) copy-start(bf16[1024,2048]{1,0:T(8,128)(2,1)} %reshape.215) | copy-start | bytes 12582916
Sparse Core Ops, SparseCore 0:
  11.6 119.8 all-gather.2
